TPU v7x, 32 devices: a whole 2x2x4 slice. The times are simulated.
32 devices in a mesh: stream: 8 (over y, x, core), wall: 4 (over z).
Axes of the slice: x: 2, y: 2, z: 4, core: 2. Of those that a mesh axis runs over, the one named last changes fastest.
Arguments:
- velocity: float32 [3, 2, 768, 2048], P(None, None, 'wall', 'stream'), may hold values from -96 to 96
- viscosity: float32 [2, 768, 2048], P(None, 'wall', 'stream'), may hold values from 2 to 4000000
- y_coef: float32 [2, 768], P(None, 'wall'), may hold values from 0.05 to 0.25
Outputs:
- updated: float32 [3, 2, 768, 2048], P(None, None, 'wall', 'stream')
All inputs are finite; a program needn't handle non-finite values.
Results may differ from a plain program's by a relative error of at most 0.0015.
Values sent between devices are 32-bit elements; how exact they have to be, the bound alone decides.
A program may use at most 64 MiB of HBM per device.

v0:
```python
import jax
import jax.numpy as jnp
from jax import lax
from jax.sharding import PartitionSpec as P

BLOCK = 16


def padded_2(x, sides, width, wrap):
    for axis, dim in sides:
        devices, length = (lax.axis_size(axis), x.shape[dim])
        up = [(i, (i + 1) % devices) for i in range(devices if wrap else devices - 1)]
        down = [(j, i) for i, j in up]
        last = lax.slice_in_dim(x, length - width, length, axis=dim)
        first = lax.slice_in_dim(x, 0, width, axis=dim)
        before = lax.ppermute(last, axis, up)
        after = lax.ppermute(first, axis, down)
        x = jnp.concatenate([before, x, after], axis=dim)
    return x


def passed_along(block, axis, distance):
    devices = range(lax.axis_size(axis))
    route = [((i - distance) % len(devices), i) for i in devices]
    return lax.ppermute(block, axis, route)


def reduce_step(middle, before, after):
    weight_lo = -middle[0] / before[1]
    weight_hi = -middle[2] / after[1]
    new_below = weight_lo * before[0]
    new_above = weight_hi * after[2]
    new_centre = middle[1] + weight_lo * before[2] + weight_hi * after[0]
    new_source = middle[3:] + weight_lo[None] * before[3:] + weight_hi[None] * after[3:]
    return jnp.concatenate([new_below[None], new_centre[None], new_above[None], new_source], axis=0)


def finish_system(system):
    return system[3:] / (system[0] + system[1] + system[2])[None]


def shards(velocity, viscosity, y_coef):
    components, planes, row_count, cell_count = velocity.shape
    block_len = BLOCK
    blocks = cell_count // block_len
    line_count = planes * row_count
    inner_len = block_len - 1
    devices_line = lax.axis_size("stream")
    padded = padded_2(velocity, (("wall", 2),), 1, False)
    coef_up = y_coef[0][None, None, :, None]
    coef_down = y_coef[1][None, None, :, None]
    source_field = (
        velocity
        + coef_up * (padded[:, :, 2:] - velocity)
        - coef_down * (velocity - padded[:, :, :-2])
    )
    stiff_rim = padded_2(viscosity, (("stream", 2),), 1, True)
    lower = -0.5 * (stiff_rim[:, :, :-2] + viscosity)
    upper = -0.5 * (viscosity + stiff_rim[:, :, 2:])
    diagonal = 1.0 - lower - upper

    def to_lanes(field):
        leading = field.shape[:-3]
        depth = len(leading)
        shaped = field.reshape(leading + (planes, row_count, blocks, block_len))
        ordering = (depth + 3,) + tuple(range(depth)) + (depth + 2, depth, depth + 1)
        return shaped.transpose(ordering).reshape((block_len,) + leading + (blocks, line_count))

    lower_l = to_lanes(lower)
    diag_l = to_lanes(diagonal)
    upper_l = to_lanes(upper)
    source_l = to_lanes(source_field)
    zeros_col = jnp.zeros((inner_len - 1, blocks, line_count), jnp.float32)
    left_col = jnp.concatenate([-lower_l[0][None], zeros_col], axis=0)
    right_col = jnp.concatenate([zeros_col, -upper_l[inner_len - 1][None]], axis=0)
    stacked = jnp.concatenate([source_l[:inner_len], left_col[:, None], right_col[:, None]], axis=1)
    ratios = []
    values = []
    ratio_prev = jnp.zeros((blocks, line_count), jnp.float32)
    value_prev = jnp.zeros((5, blocks, line_count), jnp.float32)
    for position in range(inner_len):
        denom = diag_l[position] - lower_l[position] * ratio_prev
        ratio_prev = upper_l[position] / denom
        value_prev = (stacked[position] - lower_l[position][None] * value_prev) / denom[None]
        ratios.append(ratio_prev)
        values.append(value_prev)
    solved_rows = [None] * inner_len
    following = jnp.zeros((5, blocks, line_count), jnp.float32)
    for position in reversed(range(inner_len)):
        following = values[position] - ratios[position][None] * following
        solved_rows[position] = following
    interior = jnp.stack(solved_rows, axis=0)
    heads = interior[0]
    incoming = passed_along(heads[:, 0], "stream", -1)
    nexts = jnp.concatenate([heads[:, 1:], incoming[:, None]], axis=1)
    tail = interior[inner_len - 1]
    sep_lower = lower_l[block_len - 1]
    sep_diag = diag_l[block_len - 1]
    sep_upper = upper_l[block_len - 1]
    sep_source = source_l[block_len - 1]
    below = sep_lower * tail[3]
    centre = sep_diag + sep_lower * tail[4] + sep_upper * nexts[3]
    above = sep_upper * nexts[4]
    reduced_source = sep_source - sep_lower[None] * tail[:3] - sep_upper[None] * nexts[:3]
    system = jnp.concatenate([below[None], centre[None], above[None], reduced_source], axis=0)
    for level in range(blocks.bit_length() - 1):
        stride = 1 << level
        extended = padded_2(system, (("stream", 1),), stride, True)
        before = extended[:, :blocks]
        after = extended[:, 2 * stride : 2 * stride + blocks]
        system = reduce_step(system, before, after)
    for level in range(devices_line.bit_length() - 1):
        distance = 1 << level
        before = passed_along(system, "stream", distance)
        after = passed_along(system, "stream", -distance)
        system = reduce_step(system, before, after)
    separators = finish_system(system)
    last_sep = passed_along(separators[:, blocks - 1], "stream", 1)
    previous = jnp.concatenate([last_sep[:, None], separators[:, : blocks - 1]], axis=1)
    inner_vals = (
        interior[:, :3] + interior[:, 3:4] * previous[None] + interior[:, 4:5] * separators[None]
    )
    complete = jnp.concatenate([inner_vals, separators[None]], axis=0)
    complete = complete.reshape((block_len, components, blocks, planes, row_count))
    return complete.transpose((1, 3, 4, 2, 0)).reshape((components, planes, row_count, cell_count))


def solution(mesh):
    placed = (P(None, None, "wall", "stream"), P(None, "wall", "stream"), P(None, "wall"))
    return jax.shard_map(
        shards,
        mesh=mesh,
        in_specs=placed,
        out_specs=P(None, None, "wall", "stream"),
        check_vma=False,
    )
```

profile of v0, /device:TPU:0, one launch (start us, length us, event | category | flops | bytes accessed | tf_op | source)
XLA Modules:
  0.0 101.9 jit_solution(9838464213148186563)
XLA Ops:
  0.0 1.2 %copy.234 = f32[2,192,256]{1,2,0:T(8,128)S(1)} copy(f32[2,192,256]{2,1,0:T(8,128)} %param.4) | data formatting | bytes 786432 | tf_op args[1]
  1.7 2.9 %collective-permute-start.3 = (f32[2,192,1]{1,2,0:T(1,128)S(1)}, f32[2,192,1]{1,2,0:T(1,128)S(1)}, u32[]{:S(2)}, u32[]{:S(2)}) collective-permute-start(f32[2,192,1]{1,2,0:T(1,128)S(1)} %get-tuple-element.108), channel_id=1, source_target_pairs={{4,0},{8,4},{12,8},{16,12},{20,16},{24,20},{28,24},{0,28},{5,1},{9... | collective-permute-start | bytes 4616 | tf_op jit(solution)/shard_map/ppermute | solution.py:17
  4.7 0.8 fusion.84
  6.1 4.2 %collective-permute-start.1 = (f32[3,2,1,256]{3,1,2,0:T(2,128)}, f32[3,2,1,256]{3,1,2,0:T(2,128)S(1)}, u32[]{:S(2)}, u32[]{:S(2)}) collective-permute-start(f32[3,2,1,256]{3,1,2,0:T(2,128)} %copy.302), channel_id=1, source_target_pairs={{0,1},{1,2},{2,3},{4,5},{5,6},{6,7},{8,9},{9,10},{10,11},{12,13},{... | collective-permute-start | bytes 18440 | tf_op jit(solution)/shard_map/ppermute | solution.py:16
  10.9 1.3 %collective-permute-start = (f32[3,2,1,256]{3,1,2,0:T(2,128)}, f32[3,2,1,256]{3,1,2,0:T(2,128)S(1)}, u32[]{:S(2)}, u32[]{:S(2)}) collective-permute-start(f32[3,2,1,256]{3,1,2,0:T(2,128)} %copy.301), channel_id=1, source_target_pairs={{1,0},{2,1},{3,2},{5,4},{6,5},{7,6},{9,8},{10,9},{11,10},{13,12},{... | collective-permute-start | bytes 18440 | tf_op jit(solution)/shard_map/ppermute | solution.py:17
  12.2 1.3 %fusion.90 = (f32[1,192]{1,0:T(1,128)}, f32[1,192]{1,0:T(1,128)}) fusion(f32[2,192]{1,0:T(2,128)} %param.5), kind=kLoop, calls=%fused_computation.266 | loop fusion | bytes 3072 | tf_op jit(solution)/shard_map/slice | solution.py:50
  13.5 1.7 %copy.228 = f32[3,2,192,256]{2,3,1,0:T(8,128)S(1)} copy(f32[3,2,192,256]{3,2,1,0:T(8,128)} %param.3) | data formatting | bytes 2359296 | tf_op args[0]
  16.5 0.7 slice.643
  17.2 1.1 %fusion.85 = (f32[1,16,2,192]{3,0,1,2:T(1,128)S(1)}, f32[1,16,2,192]{3,0,1,2:T(1,128)S(1)}, f32[1,16,2,192]{3,0,1,2:T(1,128)}, f32[1,16,2,192]{3,0,1,2:T(1,128)}...) fusion(f32[16,16,2,192]{3,0,1,2:T(8,128)S(1)} %bitcast.211), kind=kLoop, calls=%fused_computation.261 | loop fusion | bytes 786432 | tf_op jit(solution)/shard_map/slice | solution.py:98
  24.7 1.0 %divide_multiply_fusion = (f32[16,384]{1,0:T(8,128)S(1)}, f32[16,384]{1,0:T(8,128)S(1)}, f32[16,384]{1,0:T(8,128)S(1)}, f32[16,384]{1,0:T(8,128)}, f32[16,384]{1...) fusion(f32[16,384]{1,0:T(8,128)S(1)} %copy-done.83, ...), kind=kLoop, calls=%fused_computation.228 | loop fusion | flops 276480 | bytes 1843200 | tf_op jit(solution)/shard_map/mul | solution.py:90
  25.8 0.9 pad_bitcast_fusion
  26.8 0.7 mul.2168
  27.5 0.7 squeeze.260
  28.2 0.7 mul.2135
  28.9 0.7 squeeze.258
  29.6 0.7 squeeze.259
  30.3 1.2 %copy.230 = f32[3,2,1,256]{2,3,1,0:T(8,128)} copy(f32[3,2,1,256]{3,1,2,0:T(2,128)S(1)} %collective-permute-done.1) | data formatting | bytes 12288 | tf_op jit(solution)/shard_map/ppermute | solution.py:16
  31.5 1.2 %copy.226 = f32[3,2,1,256]{2,3,1,0:T(8,128)} copy(f32[3,2,1,256]{3,1,2,0:T(2,128)S(1)} %collective-permute-done) | data formatting | bytes 12288 | tf_op jit(solution)/shard_map/ppermute | solution.py:17
  32.7 2.5 %fusion.2 = f32[3,2,192,256]{2,3,1,0:T(8,128)S(1)} fusion(f32[3,2,192,256]{2,3,1,0:T(8,128)S(1)} %copy.228, f32[3,2,1,256]{2,3,1,0:T(8,128)} %copy.230, f32[3,2,1,256]{2,3,1,0:T(8,128)} %copy.226, f32[192]{0:T(256)S(1)} %bitcast.218, f32[192]{0:T(256)S(1)} %bitcast.217), kind=kLoop, calls=%fused_computation.4 | loop fusion | flops 2359296 | bytes 2373120 | tf_op jit(solution)/shard_map/sub | solution.py:53
  35.1 1.1 %copy.233 = f32[15,3,16,2,192]{4,3,2,1,0:T(2,128)S(1)} copy(f32[15,3,16,2,192]{4,0,2,3,1:T(8,128)S(1)} %bitcast.205) | data formatting | bytes 2211840 | tf_op jit(solution)/shard_map/slice | solution.py:76
  36.3 2.2 %slice.578 = f32[15,3,16,384]{3,2,1,0:T(8,128)} reshape(f32[15,3,16,2,192]{4,3,2,1,0:T(2,128)S(1)} %copy.233) | data formatting | bytes 2211840 | tf_op jit(solution)/shard_map/slice | solution.py:76
  38.8 1.7 %pad_maximum_fusion = f32[15,5,16,384]{3,2,1,0:T(8,128)S(1)} fusion(f32[15,1,16,384]{3,2,1,0:T(8,128)} %get-tuple-element.160, f32[15,1,16,384]{3,2,1,0:T(8,128)} %get-tuple-element.161, f32[15,3,16,384]{3,2,1,0:T(8,128)} %slice.578), kind=kLoop, calls=%fused_computation | loop fusion | flops 921600 | bytes 3686400 | tf_op jit(solution)/shard_map/concatenate | solution.py:76
  40.9 1.1 %multiply_subtract_fusion = (f32[5,16,384]{2,1,0:T(8,128)S(1)}, f32[5,16,384]{2,1,0:T(8,128)}) fusion(f32[16,384]{1,0:T(8,128)S(1)} %get-tuple-element.23, f32[16,384]{1,0:T(8,128)S(1)} %copy-done.51, f32[16,384]{1,0:T(8,128)S(1)} %get-tuple-element.27, f32[16,384]{1,0:T(8,128)S(1)} %copy-done.54, f32[16,384]{1,0:T(8,128)S(1)} %copy-done.16, ...), kind=kLoop, calls=%fused_computation.70 | loop fusion | flops 2242560 | bytes 3194880 | tf_op jit(solution)/shard_map/sub | solution.py:90
  42.0 1.9 %subtract_dynamic-update-slice_fusion = (f32[15,5,16,384]{3,2,1,0:T(8,128)S(1)}, f32[1,5,16,384]{3,2,1,0:T(8,128)S(1)}, f32[1,5,16,384]{3,2,1,0:T(8,128)S(1)}, f...) fusion(f32[16,384]{1,0:T(8,128)S(1)} %copy-done.69, ...), kind=kLoop, calls=%fused_computation.71 | loop fusion | flops 2242559 | bytes 4669440
  44.3 0.7 slice.790
  45.8 0.7 broadcast_in_dim.10
  46.5 0.9 fusion.29
  47.4 0.9 fusion.52
  48.3 2.6 %collective-permute-start.6 = (f32[6,1,384]{2,1,0:T(1,128)S(1)}, f32[6,1,384]{2,1,0:T(1,128)S(1)}, u32[]{:S(2)}, u32[]{:S(2)}) collective-permute-start(f32[6,1,384]{2,1,0:T(1,128)S(1)} %get-tuple-element.156), channel_id=1, source_target_pairs={{4,0},{8,4},{12,8},{16,12},{20,16},{24,20},{28,24},{0,28},{5,1},{9... | collective-permute-start | bytes 27656 | tf_op jit(solution)/shard_map/ppermute | solution.py:17
  50.9 1.6 %fusion.46 = f32[15,5,16,384]{3,2,1,0:T(8,128)} fusion(f32[15,5,16,384]{3,2,1,0:T(8,128)} %copy-done, f32[1,5,16,384]{3,2,1,0:T(8,128)} %get-tuple-element.15, f32[1,5,16,384]{3,2,1,0:T(8,128)} %get-tuple-element.9, f32[16,384]{1,0:T(8,128)} %get-tuple-element.35), kind=kLoop, calls=%fused_computation.140 | loop fusion | flops 61440 | bytes 393216
  52.6 3.9 %collective-permute-done.5 = f32[6,1,384]{2,1,0:T(1,128)S(1)} collective-permute-done((f32[6,1,384]{2,1,0:T(1,128)S(1)}, f32[6,1,384]{2,1,0:T(1,128)S(1)}, u32[]{:S(2)}, u32[]{:S(2)}) %collective-permute-start.5) | collective-permute-done | bytes 9248 | tf_op jit(solution)/shard_map/ppermute | solution.py:16
  58.2 3.3 %collective-permute-done.7 = f32[6,2,384]{2,1,0:T(2,128)S(1)} collective-permute-done((f32[6,2,384]{2,1,0:T(2,128)S(1)}, f32[6,2,384]{2,1,0:T(2,128)S(1)}, u32[]{:S(2)}, u32[]{:S(2)}) %collective-permute-start.7) | collective-permute-done | bytes 18464 | tf_op jit(solution)/shard_map/ppermute | solution.py:16
  63.4 3.3 %collective-permute-done.9 = f32[6,4,384]{2,1,0:T(4,128)S(1)} collective-permute-done((f32[6,4,384]{2,1,0:T(4,128)S(1)}, f32[6,4,384]{2,1,0:T(4,128)S(1)}, u32[]{:S(2)}, u32[]{:S(2)}) %collective-permute-start.9) | collective-permute-done | bytes 36896 | tf_op jit(solution)/shard_map/ppermute | solution.py:16
  68.1 1.1 %collective-permute-done.12 = f32[6,8,384]{2,1,0:T(8,128)S(1)} collective-permute-done((f32[6,8,384]{2,1,0:T(8,128)S(1)}, f32[6,8,384]{2,1,0:T(8,128)S(1)}, u32[]{:S(2)}, u32[]{:S(2)}) %collective-permute-start.12) | collective-permute-done | bytes 73760 | tf_op jit(solution)/shard_map/ppermute | solution.py:17
  69.3 3.0 %collective-permute-done.11 = f32[6,8,384]{2,1,0:T(8,128)S(1)} collective-permute-done((f32[6,8,384]{2,1,0:T(8,128)S(1)}, f32[6,8,384]{2,1,0:T(8,128)S(1)}, u32[]{:S(2)}, u32[]{:S(2)}) %collective-permute-start.11) | collective-permute-done | bytes 73760 | tf_op jit(solution)/shard_map/ppermute | solution.py:16
  74.3 2.2 %collective-permute-done.14 = f32[6,16,384]{2,1,0:T(8,128)S(1)} collective-permute-done((f32[6,16,384]{2,1,0:T(8,128)S(1)}, f32[6,16,384]{2,1,0:T(8,128)S(1)}, u32[]{:S(2)}, u32[]{:S(2)}) %collective-permute-start.14) | collective-permute-done | bytes 147488 | tf_op jit(solution)/shard_map/ppermute | solution.py:25
  76.5 1.5 %collective-permute-done.13 = f32[6,16,384]{2,1,0:T(8,128)S(1)} collective-permute-done((f32[6,16,384]{2,1,0:T(8,128)S(1)}, f32[6,16,384]{2,1,0:T(8,128)S(1)}, u32[]{:S(2)}, u32[]{:S(2)}) %collective-permute-start.13) | collective-permute-done | bytes 147488 | tf_op jit(solution)/shard_map/ppermute | solution.py:25
  78.1 1.8 %collective-permute-start.16 = (f32[6,16,384]{2,1,0:T(8,128)S(1)}, f32[6,16,384]{2,1,0:T(8,128)S(1)}, u32[]{:S(2)}, u32[]{:S(2)}) collective-permute-start(f32[6,16,384]{2,1,0:T(8,128)S(1)} %pad_maximum_fusion.12), channel_id=1, source_target_pairs={{8,0},{12,4},{16,8},{20,12},{24,16},{28,20},{0,24},{4,28},{9,1},{1... | collective-permute-start | bytes 442376 | tf_op jit(solution)/shard_map/ppermute | solution.py:25
  80.8 3.8 %collective-permute-done.16 = f32[6,16,384]{2,1,0:T(8,128)S(1)} collective-permute-done((f32[6,16,384]{2,1,0:T(8,128)S(1)}, f32[6,16,384]{2,1,0:T(8,128)S(1)}, u32[]{:S(2)}, u32[]{:S(2)}) %collective-permute-start.16) | collective-permute-done | bytes 147488 | tf_op jit(solution)/shard_map/ppermute | solution.py:25
  84.7 2.7 %collective-permute-done.15 = f32[6,16,384]{2,1,0:T(8,128)S(1)} collective-permute-done((f32[6,16,384]{2,1,0:T(8,128)S(1)}, f32[6,16,384]{2,1,0:T(8,128)S(1)}, u32[]{:S(2)}, u32[]{:S(2)}) %collective-permute-start.15) | collective-permute-done | bytes 147488 | tf_op jit(solution)/shard_map/ppermute | solution.py:25
  87.4 1.2 %collective-permute-start.17 = (f32[6,16,384]{2,1,0:T(8,128)S(1)}, f32[6,16,384]{2,1,0:T(8,128)S(1)}, u32[]{:S(2)}, u32[]{:S(2)}) collective-permute-start(f32[6,16,384]{2,1,0:T(8,128)S(1)} %pad_maximum_fusion.13), channel_id=1, source_target_pairs={{16,0},{20,4},{24,8},{28,12},{0,16},{4,20},{8,24},{12,28},{17,1},{... | collective-permute-start | bytes 442376 | tf_op jit(solution)/shard_map/ppermute | solution.py:25
  89.4 3.3 %collective-permute-done.17 = f32[6,16,384]{2,1,0:T(8,128)S(1)} collective-permute-done((f32[6,16,384]{2,1,0:T(8,128)S(1)}, f32[6,16,384]{2,1,0:T(8,128)S(1)}, u32[]{:S(2)}, u32[]{:S(2)}) %collective-permute-start.17) | collective-permute-done | bytes 147488 | tf_op jit(solution)/shard_map/ppermute | solution.py:25
  92.8 1.2 %slice_bitcast_fusion.1 = (f32[15,16,384]{2,1,0:T(8,128)S(1)}, f32[15,16,384]{2,1,0:T(8,128)S(1)}) fusion(f32[15,5,16,384]{3,2,1,0:T(8,128)} %constant_dynamic-update-slice_fusion), kind=kLoop, calls=%fused_computation.22 | loop fusion | bytes 1474560 | tf_op jit(solution)/shard_map/mul | solution.py:121
  94.2 2.5 %collective-permute-done.18 = f32[3,384]{1,0:T(4,128)S(1)} collective-permute-done((f32[3,384]{1,0:T(4,128)S(1)}, f32[3,384]{1,0:T(4,128)S(1)}, u32[]{:S(2)}, u32[]{:S(2)}) %collective-permute-start.18) | collective-permute-done | bytes 4640 | tf_op jit(solution)/shard_map/ppermute | solution.py:25
  96.8 1.4 %fusion.6 = f32[15,3,16,384]{3,2,1,0:T(8,128)S(1)} fusion(f32[15,5,16,384]{3,2,1,0:T(8,128)} %constant_dynamic-update-slice_fusion, f32[3,16,384]{2,1,0:T(8,128)S(1)} %add_divide_fusion, f32[15,16,384]{2,1,0:T(8,128)S(1)} %get-tuple-element.55, f32[3,16,384]{2,1,0:T(8,128)S(1)} %pad_maximum_fusion.14, f32[15,16,384]{2,1,0:T(8,128)S(1)} %get-tuple-element.54), kind=kLoop, calls=%fused_computation.11 | loop fusion | flops 1105920 | bytes 3096576 | tf_op jit(solution)/shard_map/add | solution.py:121
  98.2 1.0 %concatenate.110 = f32[15,3,16,2,192]{4,3,2,1,0:T(2,128)S(1)} reshape(f32[15,3,16,384]{3,2,1,0:T(8,128)S(1)} %fusion.6) | data formatting | bytes 2211840 | tf_op jit(solution)/shard_map/concatenate | solution.py:123
  99.3 0.9 copy.296
  100.4 1.5 %copy.298 = f32[3,2,192,256]{3,2,1,0:T(8,128)} copy(f32[3,2,192,256]{2,3,1,0:T(8,128)S(1)} %bitcast.207) | data formatting | bytes 2359296 | tf_op jit(solution)/shard_map/reshape | solution.py:125
  (356 shorter events, 19.6 us)
Async XLA Ops:
  1.2 14.0 %collective-permute-start.2 = (f32[2,192,1]{1,2,0:T(1,128)S(1)}, f32[2,192,1]{1,2,0:T(1,128)S(1)}, u32[]{:S(2)}, u32[]{:S(2)}) collective-permute-start(f32[2,192,1]{1,2,0:T(1,128)S(1)} %get-tuple-element.109), channel_id=1, source_target_pairs={{0,4},{4,8},{8,12},{12,16},{16,20},{20,24},{24,28},{28,0},{1,5},{5... | collective-permute-start | bytes 4616 | tf_op jit(solution)/shard_map/ppermute | solution.py:16
  1.7 13.5 %collective-permute-start.3 = (f32[2,192,1]{1,2,0:T(1,128)S(1)}, f32[2,192,1]{1,2,0:T(1,128)S(1)}, u32[]{:S(2)}, u32[]{:S(2)}) collective-permute-start(f32[2,192,1]{1,2,0:T(1,128)S(1)} %get-tuple-element.108), channel_id=1, source_target_pairs={{4,0},{8,4},{12,8},{16,12},{20,16},{24,20},{28,24},{0,28},{5,1},{9... | collective-permute-start | bytes 4616 | tf_op jit(solution)/shard_map/ppermute | solution.py:17
  6.1 24.2 %collective-permute-start.1 = (f32[3,2,1,256]{3,1,2,0:T(2,128)}, f32[3,2,1,256]{3,1,2,0:T(2,128)S(1)}, u32[]{:S(2)}, u32[]{:S(2)}) collective-permute-start(f32[3,2,1,256]{3,1,2,0:T(2,128)} %copy.302), channel_id=1, source_target_pairs={{0,1},{1,2},{2,3},{4,5},{5,6},{6,7},{8,9},{9,10},{10,11},{12,13},{... | collective-permute-start | bytes 18440 | tf_op jit(solution)/shard_map/ppermute | solution.py:16
  10.9 20.6 %collective-permute-start = (f32[3,2,1,256]{3,1,2,0:T(2,128)}, f32[3,2,1,256]{3,1,2,0:T(2,128)S(1)}, u32[]{:S(2)}, u32[]{:S(2)}) collective-permute-start(f32[3,2,1,256]{3,1,2,0:T(2,128)} %copy.301), channel_id=1, source_target_pairs={{1,0},{2,1},{3,2},{5,4},{6,5},{7,6},{9,8},{10,9},{11,10},{13,12},{... | collective-permute-start | bytes 18440 | tf_op jit(solution)/shard_map/ppermute | solution.py:17
  19.0 21.5 %copy-start.4 = (f32[16,384]{1,0:T(8,128)}, f32[16,384]{1,0:T(8,128)S(1)}, u32[]{:S(2)}) copy-start(f32[16,384]{1,0:T(8,128)S(1)} %mul.2113) | copy-start | bytes 73732
  19.4 5.2 %copy-start.18 = (f32[16,384]{1,0:T(8,128)}, f32[16,384]{1,0:T(8,128)S(1)}, u32[]{:S(2)}) copy-start(f32[16,384]{1,0:T(8,128)S(1)} %mul.2108) | copy-start | bytes 73732
  19.8 4.9 %copy-start.20 = (f32[16,384]{1,0:T(8,128)}, f32[16,384]{1,0:T(8,128)S(1)}, u32[]{:S(2)}) copy-start(f32[16,384]{1,0:T(8,128)S(1)} %mul.2103) | copy-start | bytes 73732
  20.2 4.5 %copy-start.22 = (f32[16,384]{1,0:T(8,128)}, f32[16,384]{1,0:T(8,128)S(1)}, u32[]{:S(2)}) copy-start(f32[16,384]{1,0:T(8,128)S(1)} %mul.2098) | copy-start | bytes 73732
  20.6 4.1 %copy-start.24 = (f32[16,384]{1,0:T(8,128)}, f32[16,384]{1,0:T(8,128)S(1)}, u32[]{:S(2)}) copy-start(f32[16,384]{1,0:T(8,128)S(1)} %mul.2093) | copy-start | bytes 73732
  20.9 3.8 %copy-start.83 = (f32[16,384]{1,0:T(8,128)S(1)}, f32[16,384]{1,0:T(8,128)}, u32[]{:S(2)}) copy-start(f32[16,384]{1,0:T(8,128)} %slice.643) | copy-start | bytes 73732
  21.0 4.8 %copy-start.26 = (f32[16,384]{1,0:T(8,128)}, f32[16,384]{1,0:T(8,128)S(1)}, u32[]{:S(2)}) copy-start(f32[16,384]{1,0:T(8,128)S(1)} %mul.2088) | copy-start | bytes 73732
  21.3 4.4 %copy-start.28 = (f32[16,384]{1,0:T(8,128)}, f32[16,384]{1,0:T(8,128)S(1)}, u32[]{:S(2)}) copy-start(f32[16,384]{1,0:T(8,128)S(1)} %mul.2083) | copy-start | bytes 73732
  21.7 4.0 %copy-start.30 = (f32[16,384]{1,0:T(8,128)}, f32[16,384]{1,0:T(8,128)S(1)}, u32[]{:S(2)}) copy-start(f32[16,384]{1,0:T(8,128)S(1)} %mul.2078) | copy-start | bytes 73732
  22.9 3.9 %copy-start.37 = (f32[16,384]{1,0:T(8,128)}, f32[16,384]{1,0:T(8,128)S(1)}, u32[]{:S(2)}) copy-start(f32[16,384]{1,0:T(8,128)S(1)} %mul.2063) | copy-start | bytes 73732
  24.0 6.3 %copy-start.43 = (f32[16,384]{1,0:T(8,128)}, f32[16,384]{1,0:T(8,128)S(1)}, u32[]{:S(2)}) copy-start(f32[16,384]{1,0:T(8,128)S(1)} %mul.2048) | copy-start | bytes 73732
  24.4 7.1 %copy-start.47 = (f32[16,384]{1,0:T(8,128)}, f32[16,384]{1,0:T(8,128)S(1)}, u32[]{:S(2)}) copy-start(f32[16,384]{1,0:T(8,128)S(1)} %mul.2045) | copy-start | bytes 73732
  25.8 14.7 %copy-start.6 = (f32[16,384]{1,0:T(8,128)}, f32[16,384]{1,0:T(8,128)S(1)}, u32[]{:S(2)}) copy-start(f32[16,384]{1,0:T(8,128)S(1)} %get-tuple-element.21) | copy-start | bytes 73732
  25.8 14.7 %copy-start.8 = (f32[16,384]{1,0:T(8,128)}, f32[16,384]{1,0:T(8,128)S(1)}, u32[]{:S(2)}) copy-start(f32[16,384]{1,0:T(8,128)S(1)} %get-tuple-element.22) | copy-start | bytes 73732
  25.8 14.7 %copy-start.12 = (f32[16,384]{1,0:T(8,128)}, f32[16,384]{1,0:T(8,128)S(1)}, u32[]{:S(2)}) copy-start(f32[16,384]{1,0:T(8,128)S(1)} %get-tuple-element.23) | copy-start | bytes 73732
  25.8 14.7 %copy-start.14 = (f32[16,384]{1,0:T(8,128)}, f32[16,384]{1,0:T(8,128)S(1)}, u32[]{:S(2)}) copy-start(f32[16,384]{1,0:T(8,128)S(1)} %get-tuple-element.27) | copy-start | bytes 73732
  25.8 6.9 %copy-start.84 = (f32[1,192]{1,0:T(1,128)S(1)}, f32[1,192]{1,0:T(1,128)}, u32[]{:S(2)}) copy-start(f32[1,192]{1,0:T(1,128)} %get-tuple-element.158) | copy-start | bytes 2308
  25.8 6.9 %copy-start.85 = (f32[1,192]{1,0:T(1,128)S(1)}, f32[1,192]{1,0:T(1,128)}, u32[]{:S(2)}) copy-start(f32[1,192]{1,0:T(1,128)} %get-tuple-element.159) | copy-start | bytes 2308
  43.9 1.8 %collective-permute-start.4 = (f32[5,384]{1,0:T(8,128)S(1)}, f32[5,384]{1,0:T(8,128)}, u32[]{:S(2)}, u32[]{:S(2)}) collective-permute-start(f32[5,384]{1,0:T(8,128)S(1)} %bitcast.214), channel_id=1, source_target_pairs={{4,0},{8,4},{12,8},{16,12},{20,16},{24,20},{28,24},{0,28},{5,1},{9... | collective-permute-start | bytes 23048 | tf_op jit(solution)/shard_map/ppermute | solution.py:25
  45.6 11.2 %copy-start.3 = (f32[1,5,16,384]{3,2,1,0:T(8,128)S(1)}, f32[1,5,16,384]{3,2,1,0:T(8,128)}, u32[]{:S(2)}) copy-start(f32[1,5,16,384]{3,2,1,0:T(8,128)} %get-tuple-element.9) | copy-start | bytes 368644
  48.3 4.2 %collective-permute-start.6 = (f32[6,1,384]{2,1,0:T(1,128)S(1)}, f32[6,1,384]{2,1,0:T(1,128)S(1)}, u32[]{:S(2)}, u32[]{:S(2)}) collective-permute-start(f32[6,1,384]{2,1,0:T(1,128)S(1)} %get-tuple-element.156), channel_id=1, source_target_pairs={{4,0},{8,4},{12,8},{16,12},{20,16},{24,20},{28,24},{0,28},{5,1},{9... | collective-permute-start | bytes 27656 | tf_op jit(solution)/shard_map/ppermute | solution.py:17
  52.5 4.0 %collective-permute-start.5 = (f32[6,1,384]{2,1,0:T(1,128)S(1)}, f32[6,1,384]{2,1,0:T(1,128)S(1)}, u32[]{:S(2)}, u32[]{:S(2)}) collective-permute-start(f32[6,1,384]{2,1,0:T(1,128)S(1)} %get-tuple-element.155), channel_id=1, source_target_pairs={{0,4},{4,8},{8,12},{12,16},{16,20},{20,24},{24,28},{28,0},{1,5},{5... | collective-permute-start | bytes 27656 | tf_op jit(solution)/shard_map/ppermute | solution.py:16
  52.6 9.2 %copy-start.2 = (f32[1,5,16,384]{3,2,1,0:T(8,128)S(1)}, f32[1,5,16,384]{3,2,1,0:T(8,128)}, u32[]{:S(2)}) copy-start(f32[1,5,16,384]{3,2,1,0:T(8,128)} %get-tuple-element.10) | copy-start | bytes 368644
  52.6 9.2 %copy-start.11 = (f32[1,5,16,384]{3,2,1,0:T(8,128)S(1)}, f32[1,5,16,384]{3,2,1,0:T(8,128)}, u32[]{:S(2)}) copy-start(f32[1,5,16,384]{3,2,1,0:T(8,128)} %get-tuple-element.14) | copy-start | bytes 368644
  52.6 9.2 %copy-start.17 = (f32[16,384]{1,0:T(8,128)S(1)}, f32[16,384]{1,0:T(8,128)}, u32[]{:S(2)}) copy-start(f32[16,384]{1,0:T(8,128)} %get-tuple-element.31) | copy-start | bytes 73732
  56.7 1.5 %collective-permute-start.8 = (f32[6,2,384]{2,1,0:T(2,128)S(1)}, f32[6,2,384]{2,1,0:T(2,128)S(1)}, u32[]{:S(2)}, u32[]{:S(2)}) collective-permute-start(f32[6,2,384]{2,1,0:T(2,128)S(1)} %get-tuple-element.152), channel_id=1, source_target_pairs={{4,0},{8,4},{12,8},{16,12},{20,16},{24,20},{28,24},{0,28},{5,1},{9... | collective-permute-start | bytes 55304 | tf_op jit(solution)/shard_map/ppermute | solution.py:17
  57.4 4.1 %collective-permute-start.7 = (f32[6,2,384]{2,1,0:T(2,128)S(1)}, f32[6,2,384]{2,1,0:T(2,128)S(1)}, u32[]{:S(2)}, u32[]{:S(2)}) collective-permute-start(f32[6,2,384]{2,1,0:T(2,128)S(1)} %get-tuple-element.151), channel_id=1, source_target_pairs={{0,4},{4,8},{8,12},{12,16},{16,20},{20,24},{24,28},{28,0},{1,5},{5... | collective-permute-start | bytes 55304 | tf_op jit(solution)/shard_map/ppermute | solution.py:16
  61.6 1.7 %collective-permute-start.10 = (f32[6,4,384]{2,1,0:T(4,128)S(1)}, f32[6,4,384]{2,1,0:T(4,128)S(1)}, u32[]{:S(2)}, u32[]{:S(2)}) collective-permute-start(f32[6,4,384]{2,1,0:T(4,128)S(1)} %get-tuple-element.148), channel_id=1, source_target_pairs={{4,0},{8,4},{12,8},{16,12},{20,16},{24,20},{28,24},{0,28},{5,1},{9... | collective-permute-start | bytes 110600 | tf_op jit(solution)/shard_map/ppermute | solution.py:17
  62.4 4.3 %collective-permute-start.9 = (f32[6,4,384]{2,1,0:T(4,128)S(1)}, f32[6,4,384]{2,1,0:T(4,128)S(1)}, u32[]{:S(2)}, u32[]{:S(2)}) collective-permute-start(f32[6,4,384]{2,1,0:T(4,128)S(1)} %get-tuple-element.147), channel_id=1, source_target_pairs={{0,4},{4,8},{8,12},{12,16},{16,20},{20,24},{24,28},{28,0},{1,5},{5... | collective-permute-start | bytes 110600 | tf_op jit(solution)/shard_map/ppermute | solution.py:16
  66.7 6.2 %copy-start.1 = (f32[1,5,16,384]{3,2,1,0:T(8,128)S(1)}, f32[1,5,16,384]{3,2,1,0:T(8,128)}, u32[]{:S(2)}) copy-start(f32[1,5,16,384]{3,2,1,0:T(8,128)} %get-tuple-element.11) | copy-start | bytes 368644
  66.8 6.2 %copy-start.10 = (f32[1,5,16,384]{3,2,1,0:T(8,128)S(1)}, f32[1,5,16,384]{3,2,1,0:T(8,128)}, u32[]{:S(2)}) copy-start(f32[1,5,16,384]{3,2,1,0:T(8,128)} %get-tuple-element.13) | copy-start | bytes 368644
  66.8 6.2 %copy-start.15 = (f32[16,384]{1,0:T(8,128)S(1)}, f32[16,384]{1,0:T(8,128)}, u32[]{:S(2)}) copy-start(f32[16,384]{1,0:T(8,128)} %copy-done.14) | copy-start | bytes 73732
  66.9 2.3 %collective-permute-start.12 = (f32[6,8,384]{2,1,0:T(8,128)S(1)}, f32[6,8,384]{2,1,0:T(8,128)S(1)}, u32[]{:S(2)}, u32[]{:S(2)}) collective-permute-start(f32[6,8,384]{2,1,0:T(8,128)S(1)} %get-tuple-element.144), channel_id=1, source_target_pairs={{4,0},{8,4},{12,8},{16,12},{20,16},{24,20},{28,24},{0,28},{5,1},{9... | collective-permute-start | bytes 221192 | tf_op jit(solution)/shard_map/ppermute | solution.py:17
  67.6 4.7 %collective-permute-start.11 = (f32[6,8,384]{2,1,0:T(8,128)S(1)}, f32[6,8,384]{2,1,0:T(8,128)S(1)}, u32[]{:S(2)}, u32[]{:S(2)}) collective-permute-start(f32[6,8,384]{2,1,0:T(8,128)S(1)} %get-tuple-element.143), channel_id=1, source_target_pairs={{0,4},{4,8},{8,12},{12,16},{16,20},{20,24},{24,28},{28,0},{1,5},{5... | collective-permute-start | bytes 221192 | tf_op jit(solution)/shard_map/ppermute | solution.py:16
  69.2 10.9 %copy-start.5 = (f32[16,384]{1,0:T(8,128)S(1)}, f32[16,384]{1,0:T(8,128)}, u32[]{:S(2)}) copy-start(f32[16,384]{1,0:T(8,128)} %copy-done.4) | copy-start | bytes 73732
  69.2 10.9 %copy-start.7 = (f32[16,384]{1,0:T(8,128)S(1)}, f32[16,384]{1,0:T(8,128)}, u32[]{:S(2)}) copy-start(f32[16,384]{1,0:T(8,128)} %copy-done.6) | copy-start | bytes 73732
  69.2 10.9 %copy-start.9 = (f32[16,384]{1,0:T(8,128)S(1)}, f32[16,384]{1,0:T(8,128)}, u32[]{:S(2)}) copy-start(f32[16,384]{1,0:T(8,128)} %copy-done.8) | copy-start | bytes 73732
  69.3 10.9 %copy-start.13 = (f32[16,384]{1,0:T(8,128)S(1)}, f32[16,384]{1,0:T(8,128)}, u32[]{:S(2)}) copy-start(f32[16,384]{1,0:T(8,128)} %copy-done.12) | copy-start | bytes 73732
  72.4 4.1 %collective-permute-start.14 = (f32[6,16,384]{2,1,0:T(8,128)S(1)}, f32[6,16,384]{2,1,0:T(8,128)S(1)}, u32[]{:S(2)}, u32[]{:S(2)}) collective-permute-start(f32[6,16,384]{2,1,0:T(8,128)S(1)} %pad_maximum_fusion.11), channel_id=1, source_target_pairs={{4,0},{8,4},{12,8},{16,12},{20,16},{24,20},{28,24},{0,28},{5,1},{9... | collective-permute-start | bytes 442376 | tf_op jit(solution)/shard_map/ppermute | solution.py:25
  72.5 5.5 %collective-permute-start.13 = (f32[6,16,384]{2,1,0:T(8,128)S(1)}, f32[6,16,384]{2,1,0:T(8,128)S(1)}, u32[]{:S(2)}, u32[]{:S(2)}) collective-permute-start(f32[6,16,384]{2,1,0:T(8,128)S(1)} %pad_maximum_fusion.11), channel_id=1, source_target_pairs={{28,0},{0,4},{4,8},{8,12},{12,16},{16,20},{20,24},{24,28},{29,1},{... | collective-permute-start | bytes 442376 | tf_op jit(solution)/shard_map/ppermute | solution.py:25
  78.1 6.6 %collective-permute-start.16 = (f32[6,16,384]{2,1,0:T(8,128)S(1)}, f32[6,16,384]{2,1,0:T(8,128)S(1)}, u32[]{:S(2)}, u32[]{:S(2)}) collective-permute-start(f32[6,16,384]{2,1,0:T(8,128)S(1)} %pad_maximum_fusion.12), channel_id=1, source_target_pairs={{8,0},{12,4},{16,8},{20,12},{24,16},{28,20},{0,24},{4,28},{9,1},{1... | collective-permute-start | bytes 442376 | tf_op jit(solution)/shard_map/ppermute | solution.py:25
  79.9 7.5 %collective-permute-start.15 = (f32[6,16,384]{2,1,0:T(8,128)S(1)}, f32[6,16,384]{2,1,0:T(8,128)S(1)}, u32[]{:S(2)}, u32[]{:S(2)}) collective-permute-start(f32[6,16,384]{2,1,0:T(8,128)S(1)} %pad_maximum_fusion.12), channel_id=1, source_target_pairs={{24,0},{28,4},{0,8},{4,12},{8,16},{12,20},{16,24},{20,28},{25,1},{... | collective-permute-start | bytes 442376 | tf_op jit(solution)/shard_map/ppermute | solution.py:25
  87.4 5.2 %collective-permute-start.17 = (f32[6,16,384]{2,1,0:T(8,128)S(1)}, f32[6,16,384]{2,1,0:T(8,128)S(1)}, u32[]{:S(2)}, u32[]{:S(2)}) collective-permute-start(f32[6,16,384]{2,1,0:T(8,128)S(1)} %pad_maximum_fusion.13), channel_id=1, source_target_pairs={{16,0},{20,4},{24,8},{28,12},{0,16},{4,20},{8,24},{12,28},{17,1},{... | collective-permute-start | bytes 442376 | tf_op jit(solution)/shard_map/ppermute | solution.py:25
  92.7 4.0 %collective-permute-start.18 = (f32[3,384]{1,0:T(4,128)S(1)}, f32[3,384]{1,0:T(4,128)S(1)}, u32[]{:S(2)}, u32[]{:S(2)}) collective-permute-start(f32[3,384]{1,0:T(4,128)S(1)} %bitcast.215), channel_id=1, source_target_pairs={{28,0},{0,4},{4,8},{8,12},{12,16},{16,20},{20,24},{24,28},{29,1},{... | collective-permute-start | bytes 13832 | tf_op jit(solution)/shard_map/ppermute | solution.py:25
  (57 other events, 124.4 us)
where the time goes:
time: 103 us; the launch traced here: 102 us
  local copies, waits for them, and re-layouts  33.8 us (33%)
  waiting for transfers between devices  31.5 us (31%)
  other arithmetic  17.7 us (17%)
  starting transfers between devices  17.3 us (17%)
  between operations  1.63 us (2%)
    ppermute x7, waiting for transfers between devices, passed_along(): return lax.ppermute(block, axis, route)  16 us
    ppermute x6, waiting for transfers between devices, padded_2(): before = lax.ppermute(last, axis, up)  13.5 us
    ppermute x6, starting transfers between devices, padded_2(): after = lax.ppermute(first, axis, down)  6.96 us
    unnamed x184, local copies, waits for them, and re-layouts  6.9 us
    ppermute x6, starting transfers between devices, padded_2(): before = lax.ppermute(last, axis, up)  6.13 us
    unnamed x8, other arithmetic  5.59 us
    ppermute x7, starting transfers between devices, passed_along(): return lax.ppermute(block, axis, route)  4.17 us
    slice x2, local copies, waits for them, and re-layouts, shards(): source_l[:inner_len]  3.29 us
  transfers between devices with their start and end apart: 19, of which 13 were waited for; matrix products, arithmetic and copies ran while one was open for 29% of the time, Pallas kernels for 0%

commit v1 on v0

v1 whole, which is shorter than its diff:
```python
import functools

import jax
import jax.numpy as jnp
from jax import lax
from jax.experimental import pallas as pl
from jax.experimental.pallas import tpu as pltpu
from jax.sharding import PartitionSpec as P

SEGMENTS = 8
LANES = 128
MESH = pl.DeviceIdType.MESH


def up8(rows):
    return -(-rows // 8) * 8


def join_matrix(a, b, link):
    a00, a0l, all_ = a
    b00, b0l, bll = b
    gain = link / (1.0 + link * (all_ + b00))
    left = gain * a0l
    right = gain * b0l
    return (a00 - left * a0l, left * b0l, bll - right * b0l), (gain, left, right)


def join_values(a, b, weights):
    _, left, right = weights
    jump = [al - b0 for al, b0 in zip(a[1], b[0])]
    first = [a0 - left * j for a0, j in zip(a[0], jump)]
    last = [bl + right * j for bl, j in zip(b[1], jump)]
    return (first, last), jump


def join_tree(blocks):
    levels = []
    while len(blocks) > 1:
        merged, weights = [], []
        for i in range(0, len(blocks) - 1, 2):
            (ma, fa, la), (mb, fb, lb) = blocks[i], blocks[i + 1]
            m, w = join_matrix(ma, mb, 0.5 * (la + fb))
            merged.append((m, fa, lb))
            weights.append(w)
        if len(blocks) % 2:
            merged.append(blocks[-1])
        levels.append(weights)
        blocks = merged
    return blocks[0], levels


def value_tree(values, levels):
    jumps = []
    for weights in levels:
        merged, jump = [], []
        for i, w in enumerate(weights):
            v, j = join_values(values[2 * i], values[2 * i + 1], w)
            merged.append(v)
            jump.append(j)
        if len(values) % 2:
            merged.append(values[-1])
        jumps.append(jump)
        values = merged
    return values[0], jumps


def down_tree(levels, jumps, inflow, outflow):
    flows = [(inflow, outflow)]
    for depth in reversed(range(len(levels))):
        spread = []
        for i, (gain, left, right) in enumerate(levels[depth]):
            fin, fout = flows[i]
            middle = None
            for term, weight in ((fin, left), (fout, right)):
                if term is not None:
                    part = weight if isinstance(term, float) else term * weight
                    middle = part if middle is None else middle + part
            if jumps is not None:
                part = gain * jumps[depth][i]
                middle = part if middle is None else middle + part
            spread += [(fin, middle), (middle, fout)]
        flows = spread
    return flows


def kernel(devices, wall_devices, planes, vel, visc, coef, out,
           rows_out, rows_in, stiff_t, src, src_t, ratio_s, inv_s, head_s, y_s, seg, flow,
           sol_t, sol, coef_s, ring_s, msg_a, msg_b, got_a, got_b,
           wall_send, wall_recv, a_send, a_recv, b_send, b_recv):
    components, lines, cells = vel.shape
    rows = lines // planes
    groups = lines // LANES
    length = cells // SEGMENTS
    me = lax.axis_index("stream")
    wall = lax.axis_index("wall")
    has_below = wall > 0
    has_above = wall < wall_devices - 1

    barrier = pltpu.get_barrier_semaphore()
    for d in range(1, devices):
        pl.semaphore_signal(barrier, inc=1, device_id={"stream": lax.rem(me + d, devices)}, device_id_type=MESH)

    @pl.when(has_below)
    def _():
        pl.semaphore_signal(barrier, inc=1, device_id={"wall": wall - 1}, device_id_type=MESH)

    @pl.when(has_above)
    def _():
        pl.semaphore_signal(barrier, inc=1, device_id={"wall": wall + 1}, device_id_type=MESH)

    for c in range(components):
        for p in range(planes):
            at = c * planes + p
            rows_out[0, at : at + 1, :] = vel[c, p * rows + rows - 1 : p * rows + rows, :]
            rows_out[1, at : at + 1, :] = vel[c, p * rows : p * rows + 1, :]

    beside = jnp.where(has_below, 1, 0) + jnp.where(has_above, 1, 0)
    pl.semaphore_wait(barrier, devices - 1 + beside)

    def wall_copy(side, target):
        return pltpu.make_async_remote_copy(
            src_ref=rows_out.at[side], dst_ref=rows_in.at[side],
            send_sem=wall_send.at[side], recv_sem=wall_recv.at[side],
            device_id={"wall": target}, device_id_type=MESH)

    @pl.when(has_above)
    def _():
        wall_copy(0, wall + 1).start()

    @pl.when(has_below)
    def _():
        wall_copy(1, wall - 1).start()

    @pl.when(jnp.logical_not(has_below))
    def _():
        rows_in[0] = jnp.zeros(rows_in.shape[1:], jnp.float32)

    @pl.when(jnp.logical_not(has_above))
    def _():
        rows_in[1] = jnp.zeros(rows_in.shape[1:], jnp.float32)

    def ring_copy(d, source, target, send, recv):
        return pltpu.make_async_remote_copy(
            src_ref=source, dst_ref=target.at[d - 1],
            send_sem=send.at[d - 1], recv_sem=recv.at[d - 1],
            device_id={"stream": lax.rem(me + d, devices)}, device_id_type=MESH)

    def at_position(i):
        return pl.ds(i, SEGMENTS, stride=length)

    def put_segments(slot, value):
        for g in range(groups):
            seg[slot, pl.ds(g, SEGMENTS, stride=8), :] = value[g]

    def take_segment(slot, s):
        return seg[slot, s * 8 : s * 8 + groups, :]

    for g in range(groups):
        stiff_t[g] = visc[g * LANES : (g + 1) * LANES, :].T

    one = jnp.ones((groups, SEGMENTS, LANES), jnp.float32)
    excess = one
    reach = one
    first_first = jnp.zeros_like(one)
    stiff = stiff_t[:, at_position(0), :]
    first_stiff = stiff
    for i in range(length):
        if i < length - 1:
            following = stiff_t[:, at_position(i + 1), :]
            link = 0.5 * (stiff + following)
            stiff = following
            inv = 1.0 / (excess + link)
            ratio = link * inv
            ratio_s[i] = ratio
        else:
            inv = 1.0 / excess
        head = reach * inv
        inv_s[i] = inv
        head_s[i] = head
        first_first = first_first + head * reach
        if i < length - 1:
            excess = 1.0 + ratio * excess
            reach = reach * ratio
    for slot, value in enumerate((first_first, head, inv, first_stiff, stiff)):
        put_segments(slot, value)
    blocks = []
    for s in range(SEGMENTS):
        v = [take_segment(slot, s) for slot in range(5)]
        blocks.append((tuple(v[:3]), v[3], v[4]))
    mine, levels = join_tree(blocks)
    for q, value in enumerate(mine[0] + (mine[1], mine[2])):
        msg_a[q * groups : (q + 1) * groups, :] = value
    for d in range(1, devices):
        ring_copy(d, msg_a, got_a, a_send, a_recv).start()

    coef_s[...] = jnp.zeros(coef_s.shape, jnp.float32)
    coef_s[0:2, 0:rows] = coef[...]
    turned = coef_s[...].T
    toward_up = turned[0:rows, 0:1]
    toward_down = turned[0:rows, 1:2]
    keep = 1.0 - toward_up - toward_down
    row_of = lax.broadcasted_iota(jnp.int32, (rows, cells), 0)

    @pl.when(has_below)
    def _():
        wall_copy(0, wall).wait_recv()

    @pl.when(has_above)
    def _():
        wall_copy(1, wall).wait_recv()

    for c in range(components):
        for p in range(planes):
            at = c * planes + p
            v = vel[c, p * rows : (p + 1) * rows, :]
            above = jnp.where(row_of == rows - 1, rows_in[1, at : at + 1, :], pltpu.roll(v, rows - 1, 0))
            below = jnp.where(row_of == 0, rows_in[0, at : at + 1, :], pltpu.roll(v, 1, 0))
            src[c, p * rows : (p + 1) * rows, :] = v + toward_up * (above - v) - toward_down * (v - below)
        for g in range(groups):
            src_t[c, g] = src[c, g * LANES : (g + 1) * LANES, :].T

    y = [None] * components
    first = [None] * components
    for i in range(length):
        head = head_s[i]
        for c in range(components):
            f = src_t[c, :, at_position(i), :]
            y[c] = f if i == 0 else f + ratio_s[i - 1] * y[c]
            y_s[c, i] = y[c]
            first[c] = head * y[c] if i == 0 else first[c] + head * y[c]
    inv = inv_s[length - 1]
    for c in range(components):
        put_segments(c, first[c])
        put_segments(components + c, inv * y[c])
    values = []
    for s in range(SEGMENTS):
        v = [take_segment(slot, s) for slot in range(2 * components)]
        values.append((v[:components], v[components:]))
    own, jumps = value_tree(values, levels)
    for q, value in enumerate(own[0] + own[1]):
        msg_b[q * groups : (q + 1) * groups, :] = value
    for d in range(1, devices):
        ring_copy(d, msg_b, got_b, b_send, b_recv).start()

    fields = components + 2
    zero = jnp.zeros((groups, LANES), jnp.float32)
    unit = jnp.ones((groups, LANES), jnp.float32)
    for f in range(fields):
        if f < components:
            picked = [[j[f] for j in level] for level in jumps]
            flows = down_tree(levels, picked, None, None)
        elif f == components:
            flows = down_tree(levels, None, 1.0, None)
        else:
            flows = down_tree(levels, None, None, 1.0)
        for s, (fin, fout) in enumerate(flows):
            for side, term in enumerate((fin, fout)):
                term = zero if term is None else unit if isinstance(term, float) else term
                seg[2 * f + side, s * 8 : s * 8 + groups, :] = term
    fin, fout = [], []
    for f in range(fields):
        for slot, into in ((2 * f, fin), (2 * f + 1, fout)):
            into.append(jnp.stack([seg[slot, pl.ds(g, SEGMENTS, stride=8), :] for g in range(groups)]))
    now = [None] * fields
    for i in reversed(range(length)):
        head = head_s[i]
        inv = inv_s[i]
        if i < length - 1:
            ratio = ratio_s[i]
        for f in range(fields):
            value = fin[f] * head
            if f < components:
                value = value + y_s[f, i] * inv
            if i < length - 1:
                value = value + ratio * now[f]
            else:
                value = value - fout[f] * inv
            now[f] = value
            sol_t[f, :, at_position(i), :] = value
    for f in range(fields):
        for g in range(groups):
            sol[f, g * LANES : (g + 1) * LANES, :] = sol_t[f, g].T

    for d in range(1, devices):
        ring_copy(d, msg_a, got_a, a_send, a_recv).wait()
    others = []
    for t in range(1, devices):
        slot = devices - t - 1
        v = [got_a[slot, q * groups : (q + 1) * groups, :] for q in range(5)]
        others.append((tuple(v[:3]), v[3], v[4]))
    rest, ring_levels = join_tree(others)
    (m00, m0l, mll), m_first, m_last = mine
    (b00, b0l, bll), b_first, b_last = rest
    out_diag = 2.0 / (m_last + b_first) + mll + b00
    in_diag = 2.0 / (b_last + m_first) + bll + m00
    cross = m0l + b0l
    det = 1.0 / (out_diag * in_diag - cross * cross)

    for d in range(1, devices):
        ring_copy(d, msg_b, got_b, b_send, b_recv).wait()
    theirs = []
    for t in range(1, devices):
        slot = devices - t - 1
        v = [got_b[slot, q * groups : (q + 1) * groups, :] for q in range(2 * components)]
        theirs.append((v[:components], v[components:]))
    tail, _ = value_tree(theirs, ring_levels)
    for c in range(components):
        gap_out = own[1][c] - tail[0][c]
        gap_in = tail[1][c] - own[0][c]
        outflow = (in_diag * gap_out + cross * gap_in) * det
        inflow = (out_diag * gap_in + cross * gap_out) * det
        for g in range(groups):
            flow[g, c : c + 1, :] = inflow[g : g + 1]
            flow[g, components + c : components + c + 1, :] = outflow[g : g + 1]

    for g in range(groups):
        span = slice(g * LANES, (g + 1) * LANES)
        columns = flow[g].T
        from_left = sol[components, span, :]
        from_right = sol[components + 1, span, :]
        for c in range(components):
            out[c, span, :] = (
                sol[c, span, :]
                + columns[:, c : c + 1] * from_left
                + columns[:, components + c : components + c + 1] * from_right
            )

    @pl.when(has_above)
    def _():
        wall_copy(0, wall + 1).wait_send()

    @pl.when(has_below)
    def _():
        wall_copy(1, wall - 1).wait_send()


def shards(devices, wall_devices, velocity, viscosity, y_coef):
    components, planes, rows, cells = velocity.shape
    lines = planes * rows
    groups = lines // LANES
    length = cells // SEGMENTS
    fields = components + 2
    f32 = jnp.float32
    edge = up8(components * planes)
    rows_a, rows_b = up8(5 * groups), up8(2 * components * groups)
    peers = devices - 1
    tiles = (groups, SEGMENTS, LANES)
    flipped = (groups, cells, LANES)
    vmem = pl.BlockSpec(memory_space=pltpu.VMEM)
    result = pl.pallas_call(
        functools.partial(kernel, devices, wall_devices, planes),
        out_shape=jax.ShapeDtypeStruct((components, lines, cells), f32),
        in_specs=[vmem] * 3,
        out_specs=vmem,
        scratch_shapes=[
            pltpu.VMEM((2, edge, cells), f32),
            pltpu.VMEM((2, edge, cells), f32),
            pltpu.VMEM(flipped, f32),
            pltpu.VMEM((components, lines, cells), f32),
            pltpu.VMEM((components,) + flipped, f32),
            pltpu.VMEM((length,) + tiles, f32),
            pltpu.VMEM((length,) + tiles, f32),
            pltpu.VMEM((length,) + tiles, f32),
            pltpu.VMEM((components, length) + tiles, f32),
            pltpu.VMEM((2 * fields, SEGMENTS * 8, LANES), f32),
            pltpu.VMEM((groups, up8(2 * components), LANES), f32),
            pltpu.VMEM((fields,) + flipped, f32),
            pltpu.VMEM((fields, lines, cells), f32),
            pltpu.VMEM((8, -(-rows // LANES) * LANES), f32),
            pltpu.VMEM((8, LANES), f32),
            pltpu.VMEM((rows_a, LANES), f32),
            pltpu.VMEM((rows_b, LANES), f32),
            pltpu.VMEM((peers, rows_a, LANES), f32),
            pltpu.VMEM((peers, rows_b, LANES), f32),
            pltpu.SemaphoreType.DMA((2,)),
            pltpu.SemaphoreType.DMA((2,)),
            pltpu.SemaphoreType.DMA((peers,)),
            pltpu.SemaphoreType.DMA((peers,)),
            pltpu.SemaphoreType.DMA((peers,)),
            pltpu.SemaphoreType.DMA((peers,)),
        ],
        compiler_params=pltpu.CompilerParams(
            collective_id=0, has_side_effects=True, vmem_limit_bytes=40 * 1024 * 1024
        ),
        name="implicit_lines",
    )(
        velocity.reshape(components, lines, cells),
        viscosity.reshape(lines, cells),
        y_coef,
    )
    return result.reshape(velocity.shape)


def solution(mesh):
    placed = (P(None, None, "wall", "stream"), P(None, "wall", "stream"), P(None, "wall"))
    return jax.shard_map(
        functools.partial(shards, mesh.shape["stream"], mesh.shape["wall"]),
        mesh=mesh,
        in_specs=placed,
        out_specs=P(None, None, "wall", "stream"),
        check_vma=False,
    )
```

time: 103 us -> 16.5 us (0.16)
  waiting for transfers between devices: 31.5 us -> 0 us
  local copies, waits for them, and re-layouts: 33.8 us -> 3.96 us
  other arithmetic: 17.7 us -> 0 us
  starting transfers between devices: 17.3 us -> 0 us
  Pallas kernels: 0 us -> 12.4 us
  between operations: 1.63 us -> 0.01 us
    ppermute x19 -> x0, waiting for transfers between devices: 31.5 us -> none  [the longest x7 16 us: passed_along(): return lax.ppermute(block, axis, route)]
    ppermute x19 -> x0, starting transfers between devices: 17.3 us -> none  [the longest x6 6.96 us: padded_2(): after = lax.ppermute(first, axis, down)]
    pallas_call x0 -> x1, Pallas kernels: none -> 12.4 us  [shards(): pl.pallas_call(functools.partial(kernel, devices, wall_devices, planes),...]
    slice x60 -> x0, local copies, waits for them, and re-layouts: 9.49 us -> none  [the longest x2 3.29 us: shards(): source_l[:inner_len]]
    unnamed x8 -> x0, other arithmetic: 5.59 us -> none
    squeeze x33 -> x0, local copies, waits for them, and re-layouts: 4.94 us -> none  [the longest x15 1.43 us: shards(): denom = diag_l[position] - lower_l[position] * ratio_prev]
    sub x4 -> x0, other arithmetic: 4.67 us -> none  [the longest x1 2.45 us: shards(): velocity + coef_up * (padded[:, :, 2:] - velocity)]
    mul x19 -> x0, local copies, waits for them, and re-layouts: 4 us -> none  [the longest x16 1.46 us: shards(): lower_l[position][None] * value_prev]
  transfers between devices with their start and end apart: 19 -> 0, of which waited for: 13 -> 0; matrix products, arithmetic and copies ran while one was open for 29% -> 0% of each run, Pallas kernels for 0% -> 0%
where the time goes in v1:
time: 16.5 us; the launch traced here: 16.3 us
  Pallas kernels  12.4 us (75%)
  local copies, waits for them, and re-layouts  3.96 us (24%)
    pallas_call x1, Pallas kernels, shards(): pl.pallas_call(functools.partial(kernel, devices, wall_devices, planes),...  12.4 us
    unnamed x7, local copies, waits for them, and re-layouts  3.96 us

profile of v1, /device:TPU:0, one launch (start us, length us, event | category | flops | bytes accessed | tf_op | source)
XLA Modules:
  0.0 16.3 jit_solution(7218095998977472126)
XLA Ops:
  0.0 0.0 copy-start
  0.0 1.3 %copy-done = f32[3,2,192,256]{3,2,1,0:T(8,128)S(1)} copy-done((f32[3,2,192,256]{3,2,1,0:T(8,128)S(1)}, f32[3,2,192,256]{3,2,1,0:T(8,128)}, u32[]{:S(2)}) %copy-start) | copy-done | bytes 1179672
  1.3 0.0 copy-start.1
  1.3 1.0 %copy-done.1 = f32[2,192,256]{2,1,0:T(8,128)S(1)} copy-done((f32[2,192,256]{2,1,0:T(8,128)S(1)}, f32[2,192,256]{2,1,0:T(8,128)}, u32[]{:S(2)}) %copy-start.1) | copy-done | bytes 393240
  2.3 0.0 copy-start.2
  2.3 0.7 %copy-done.2 = f32[2,192]{1,0:T(2,128)S(1)} copy-done((f32[2,192]{1,0:T(2,128)S(1)}, f32[2,192]{1,0:T(2,128)}, u32[]{:S(2)}) %copy-start.2) | copy-done | bytes 1560
  3.0 12.4 %implicit_lines.1 = f32[3,384,256]{2,1,0:T(8,128)S(1)} custom-call(f32[3,384,256]{2,1,0:T(8,128)S(1)} %bitcast.4, f32[384,256]{1,0:T(8,128)S(1)} %bitcast.5, f32[2,192]{1,0:T(2,128)S(1)} %copy-done.2), custom_call_target="tpu_custom_call" | custom-call | tf_op jit(solution)/shard_map/implicit_lines/pallas_call | solution.py:350
  15.3 1.0 %copy.5 = f32[3,2,192,256]{3,2,1,0:T(8,128)} copy(f32[3,2,192,256]{3,2,1,0:T(8,128)S(1)} %bitcast.3) | data formatting | bytes 2359296
Async XLA Ops:
  0.0 1.3 %copy-start = (f32[3,2,192,256]{3,2,1,0:T(8,128)S(1)}, f32[3,2,192,256]{3,2,1,0:T(8,128)}, u32[]{:S(2)}) copy-start(f32[3,2,192,256]{3,2,1,0:T(8,128)} %param.3) | copy-start | bytes 3538948
  1.3 1.0 %copy-start.1 = (f32[2,192,256]{2,1,0:T(8,128)S(1)}, f32[2,192,256]{2,1,0:T(8,128)}, u32[]{:S(2)}) copy-start(f32[2,192,256]{2,1,0:T(8,128)} %param.4) | copy-start | bytes 1179652
  2.3 0.7 %copy-start.2 = (f32[2,192]{1,0:T(2,128)S(1)}, f32[2,192]{1,0:T(2,128)}, u32[]{:S(2)}) copy-start(f32[2,192]{1,0:T(2,128)} %coef.1) | copy-start | bytes 4612

commit v2 on v1

--- a/solution.py
+++ b/solution.py
@@ -83,10 +83,10 @@
     return flows
 
 
-def kernel(devices, wall_devices, planes, vel, visc, coef, out,
-           rows_out, rows_in, stiff_t, src, src_t, ratio_s, inv_s, head_s, y_s, seg, flow,
-           sol_t, sol, coef_s, ring_s, msg_a, msg_b, got_a, got_b,
-           wall_send, wall_recv, a_send, a_recv, b_send, b_recv):
+def kernel(devices, wall_devices, planes, vel_hbm, visc_hbm, coef_hbm, out,
+           vel, visc, coef, rows_out, rows_in, rim, stiff_t, src, src_t, rim_t, ratio_s, inv_s, head_s,
+           y_s, rim_y, seg, flow, sol_t, sol, coef_s, msg_a, msg_b, msg_c, got_a, got_b, got_c, load_sem,
+           wall_send, wall_recv, a_send, a_recv, b_send, b_recv, c_send, c_recv):
     components, lines, cells = vel.shape
     rows = lines // planes
     groups = lines // LANES
@@ -108,12 +108,26 @@
     def _():
         pl.semaphore_signal(barrier, inc=1, device_id={"wall": wall + 1}, device_id_type=MESH)
 
-    for c in range(components):
-        for p in range(planes):
-            at = c * planes + p
-            rows_out[0, at : at + 1, :] = vel[c, p * rows + rows - 1 : p * rows + rows, :]
-            rows_out[1, at : at + 1, :] = vel[c, p * rows : p * rows + 1, :]
-
+    loads = [
+        pltpu.make_async_copy(source, target, load_sem.at[i])
+        for i, (source, target) in enumerate(((visc_hbm, visc), (vel_hbm, vel), (coef_hbm, coef)))
+    ]
+    for load in loads:
+        load.start()
+    bounds = [(c * planes + p, c, p * rows, (p + 1) * rows - 1) for c in range(components) for p in range(planes)]
+    loads[0].wait()
+    rim[...] = jnp.ones(rim.shape, jnp.float32)
+    for at, c, low, high in bounds:
+        rim[at : at + 1, :] = visc[low : low + 1, :]
+        rim[8 + at : 9 + at, :] = visc[high : high + 1, :]
+    for g in range(groups):
+        stiff_t[g] = visc[g * LANES : (g + 1) * LANES, :].T
+    stiff_t[groups] = rim[...].T
+
+    loads[1].wait()
+    for at, c, low, high in bounds:
+        rows_out[0, at : at + 1, :] = vel[c, high : high + 1, :]
+        rows_out[1, at : at + 1, :] = vel[c, low : low + 1, :]
     beside = jnp.where(has_below, 1, 0) + jnp.where(has_above, 1, 0)
     pl.semaphore_wait(barrier, devices - 1 + beside)
 
@@ -148,17 +162,16 @@
     def at_position(i):
         return pl.ds(i, SEGMENTS, stride=length)
 
-    def put_segments(slot, value):
-        for g in range(groups):
-            seg[slot, pl.ds(g, SEGMENTS, stride=8), :] = value[g]
-
-    def take_segment(slot, s):
-        return seg[slot, s * 8 : s * 8 + groups, :]
-
-    for g in range(groups):
-        stiff_t[g] = visc[g * LANES : (g + 1) * LANES, :].T
-
-    one = jnp.ones((groups, SEGMENTS, LANES), jnp.float32)
+    every = groups + 1
+
+    def put_segments(slot, value, first_group=0):
+        for g in range(value.shape[0]):
+            seg[slot, pl.ds(first_group + g, SEGMENTS, stride=8), :] = value[g]
+
+    def take_segment(slot, s, span=slice(0, groups)):
+        return seg[slot, s * 8 + span.start : s * 8 + span.stop, :]
+
+    one = jnp.ones((every, SEGMENTS, LANES), jnp.float32)
     excess = one
     reach = one
     first_first = jnp.zeros_like(one)
@@ -185,14 +198,20 @@
         put_segments(slot, value)
     blocks = []
     for s in range(SEGMENTS):
-        v = [take_segment(slot, s) for slot in range(5)]
+        v = [take_segment(slot, s, slice(0, every)) for slot in range(5)]
         blocks.append((tuple(v[:3]), v[3], v[4]))
     mine, levels = join_tree(blocks)
     for q, value in enumerate(mine[0] + (mine[1], mine[2])):
-        msg_a[q * groups : (q + 1) * groups, :] = value
+        msg_a[q * every : (q + 1) * every, :] = value
     for d in range(1, devices):
         ring_copy(d, msg_a, got_a, a_send, a_recv).start()
 
+    def part(levels, span):
+        return [[tuple(w[span] for w in weights) for weights in level] for level in levels]
+
+    main, last = slice(0, groups), slice(groups, every)
+    main_levels, rim_levels = part(levels, main), part(levels, last)
+    loads[2].wait()
     coef_s[...] = jnp.zeros(coef_s.shape, jnp.float32)
     coef_s[0:2, 0:rows] = coef[...]
     turned = coef_s[...].T
@@ -201,20 +220,11 @@
     keep = 1.0 - toward_up - toward_down
     row_of = lax.broadcasted_iota(jnp.int32, (rows, cells), 0)
 
-    @pl.when(has_below)
-    def _():
-        wall_copy(0, wall).wait_recv()
-
-    @pl.when(has_above)
-    def _():
-        wall_copy(1, wall).wait_recv()
-
     for c in range(components):
         for p in range(planes):
-            at = c * planes + p
             v = vel[c, p * rows : (p + 1) * rows, :]
-            above = jnp.where(row_of == rows - 1, rows_in[1, at : at + 1, :], pltpu.roll(v, rows - 1, 0))
-            below = jnp.where(row_of == 0, rows_in[0, at : at + 1, :], pltpu.roll(v, 1, 0))
+            above = jnp.where(row_of == rows - 1, 0.0, pltpu.roll(v, rows - 1, 0))
+            below = jnp.where(row_of == 0, 0.0, pltpu.roll(v, 1, 0))
             src[c, p * rows : (p + 1) * rows, :] = v + toward_up * (above - v) - toward_down * (v - below)
         for g in range(groups):
             src_t[c, g] = src[c, g * LANES : (g + 1) * LANES, :].T
@@ -222,13 +232,13 @@
     y = [None] * components
     first = [None] * components
     for i in range(length):
-        head = head_s[i]
+        head = head_s[i, main]
         for c in range(components):
             f = src_t[c, :, at_position(i), :]
-            y[c] = f if i == 0 else f + ratio_s[i - 1] * y[c]
+            y[c] = f if i == 0 else f + ratio_s[i - 1, main] * y[c]
             y_s[c, i] = y[c]
             first[c] = head * y[c] if i == 0 else first[c] + head * y[c]
-    inv = inv_s[length - 1]
+    inv = inv_s[length - 1, main]
     for c in range(components):
         put_segments(c, first[c])
         put_segments(components + c, inv * y[c])
@@ -236,11 +246,40 @@
     for s in range(SEGMENTS):
         v = [take_segment(slot, s) for slot in range(2 * components)]
         values.append((v[:components], v[components:]))
-    own, jumps = value_tree(values, levels)
+    own, jumps = value_tree(values, main_levels)
     for q, value in enumerate(own[0] + own[1]):
         msg_b[q * groups : (q + 1) * groups, :] = value
     for d in range(1, devices):
         ring_copy(d, msg_b, got_b, b_send, b_recv).start()
+
+    @pl.when(has_below)
+    def _():
+        wall_copy(0, wall).wait_recv()
+
+    @pl.when(has_above)
+    def _():
+        wall_copy(1, wall).wait_recv()
+
+    rim[0:8, :] = rows_in[0] * turned[0:1, 1:2]
+    rim[8:16, :] = rows_in[1] * turned[rows - 1 : rows, 0:1]
+    rim_t[...] = rim[...].T
+    for i in range(length):
+        f = rim_t[at_position(i), :]
+        head = head_s[i, groups]
+        edge = f if i == 0 else f + ratio_s[i - 1, groups] * edge
+        rim_y[i] = edge
+        edge_first = head * edge if i == 0 else edge_first + head * edge
+    put_segments(0, edge_first[None], groups)
+    put_segments(1, (inv_s[length - 1, groups] * edge)[None], groups)
+    values = []
+    for s in range(SEGMENTS):
+        v = [take_segment(slot, s, last) for slot in range(2)]
+        values.append((v[:1], v[1:]))
+    rim_own, rim_jumps = value_tree(values, rim_levels)
+    msg_c[0:1, :] = rim_own[0][0]
+    msg_c[1:2, :] = rim_own[1][0]
+    for d in range(1, devices):
+        ring_copy(d, msg_c, got_c, c_send, c_recv).start()
 
     fields = components + 2
     zero = jnp.zeros((groups, LANES), jnp.float32)
@@ -248,11 +287,11 @@
     for f in range(fields):
         if f < components:
             picked = [[j[f] for j in level] for level in jumps]
-            flows = down_tree(levels, picked, None, None)
+            flows = down_tree(main_levels, picked, None, None)
         elif f == components:
-            flows = down_tree(levels, None, 1.0, None)
+            flows = down_tree(main_levels, None, 1.0, None)
         else:
-            flows = down_tree(levels, None, None, 1.0)
+            flows = down_tree(main_levels, None, None, 1.0)
         for s, (fin, fout) in enumerate(flows):
             for side, term in enumerate((fin, fout)):
                 term = zero if term is None else unit if isinstance(term, float) else term
@@ -261,12 +300,27 @@
     for f in range(fields):
         for slot, into in ((2 * f, fin), (2 * f + 1, fout)):
             into.append(jnp.stack([seg[slot, pl.ds(g, SEGMENTS, stride=8), :] for g in range(groups)]))
+    picked = [[j[0] for j in level] for level in rim_jumps]
+    for s, terms in enumerate(down_tree(rim_levels, picked, None, None)):
+        for side, term in enumerate(terms):
+            term = jnp.zeros((1, LANES), jnp.float32) if term is None else term
+            seg[side, s * 8 + groups : s * 8 + every, :] = term
+    rim_fin, rim_fout = (seg[side, pl.ds(groups, SEGMENTS, stride=8), :] for side in range(2))
+    for i in reversed(range(length)):
+        value = rim_fin * head_s[i, groups] + rim_y[i] * inv_s[i, groups]
+        if i < length - 1:
+            value = value + ratio_s[i, groups] * edge
+        else:
+            value = value - rim_fout * inv_s[i, groups]
+        edge = value
+        rim_t[at_position(i), :] = edge
+    rim[...] = rim_t[...].T
     now = [None] * fields
     for i in reversed(range(length)):
-        head = head_s[i]
-        inv = inv_s[i]
+        head = head_s[i, main]
+        inv = inv_s[i, main]
         if i < length - 1:
-            ratio = ratio_s[i]
+            ratio = ratio_s[i, main]
         for f in range(fields):
             value = fin[f] * head
             if f < components:
@@ -286,7 +340,7 @@
     others = []
     for t in range(1, devices):
         slot = devices - t - 1
-        v = [got_a[slot, q * groups : (q + 1) * groups, :] for q in range(5)]
+        v = [got_a[slot, q * every : (q + 1) * every, :] for q in range(5)]
         others.append((tuple(v[:3]), v[3], v[4]))
     rest, ring_levels = join_tree(others)
     (m00, m0l, mll), m_first, m_last = mine
@@ -296,6 +350,13 @@
     cross = m0l + b0l
     det = 1.0 / (out_diag * in_diag - cross * cross)
 
+    def end_flows(mine_ends, other_ends, span):
+        gap_out = mine_ends[1] - other_ends[0]
+        gap_in = other_ends[1] - mine_ends[0]
+        outflow = (in_diag[span] * gap_out + cross[span] * gap_in) * det[span]
+        inflow = (out_diag[span] * gap_in + cross[span] * gap_out) * det[span]
+        return inflow, outflow
+
     for d in range(1, devices):
         ring_copy(d, msg_b, got_b, b_send, b_recv).wait()
     theirs = []
@@ -303,12 +364,9 @@
         slot = devices - t - 1
         v = [got_b[slot, q * groups : (q + 1) * groups, :] for q in range(2 * components)]
         theirs.append((v[:components], v[components:]))
-    tail, _ = value_tree(theirs, ring_levels)
+    tail, _ = value_tree(theirs, part(ring_levels, main))
     for c in range(components):
-        gap_out = own[1][c] - tail[0][c]
-        gap_in = tail[1][c] - own[0][c]
-        outflow = (in_diag * gap_out + cross * gap_in) * det
-        inflow = (out_diag * gap_in + cross * gap_out) * det
+        inflow, outflow = end_flows((own[0][c], own[1][c]), (tail[0][c], tail[1][c]), main)
         for g in range(groups):
             flow[g, c : c + 1, :] = inflow[g : g + 1]
             flow[g, components + c : components + c + 1, :] = outflow[g : g + 1]
@@ -325,6 +383,26 @@
                 + columns[:, components + c : components + c + 1] * from_right
             )
 
+    for d in range(1, devices):
+        ring_copy(d, msg_c, got_c, c_send, c_recv).wait()
+    theirs = []
+    for t in range(1, devices):
+        slot = devices - t - 1
+        theirs.append(([got_c[slot, 0:1, :]], [got_c[slot, 1:2, :]]))
+    tail, _ = value_tree(theirs, part(ring_levels, last))
+    inflow, outflow = end_flows((rim_own[0][0], rim_own[1][0]), (tail[0][0], tail[1][0]), last)
+    flow[0, 0:1, :] = inflow
+    flow[0, 1:2, :] = outflow
+    columns = flow[0].T
+    for at, c, low, high in bounds:
+        for e, r in ((at, low), (8 + at, high)):
+            out[c, r : r + 1, :] = (
+                out[c, r : r + 1, :]
+                + rim[e : e + 1, :]
+                + columns[e : e + 1, 0:1] * sol[components, r : r + 1, :]
+                + columns[e : e + 1, 1:2] * sol[components + 1, r : r + 1, :]
+            )
+
     @pl.when(has_above)
     def _():
         wall_copy(0, wall + 1).wait_send()
@@ -341,8 +419,8 @@
     length = cells // SEGMENTS
     fields = components + 2
     f32 = jnp.float32
-    edge = up8(components * planes)
-    rows_a, rows_b = up8(5 * groups), up8(2 * components * groups)
+    every = groups + 1
+    rows_a, rows_b = up8(5 * every), up8(2 * components * groups)
     peers = devices - 1
     tiles = (groups, SEGMENTS, LANES)
     flipped = (groups, cells, LANES)
@@ -350,43 +428,47 @@
     result = pl.pallas_call(
         functools.partial(kernel, devices, wall_devices, planes),
         out_shape=jax.ShapeDtypeStruct((components, lines, cells), f32),
-        in_specs=[vmem] * 3,
+        in_specs=[pl.BlockSpec(memory_space=pltpu.HBM)] * 3,
         out_specs=vmem,
         scratch_shapes=[
-            pltpu.VMEM((2, edge, cells), f32),
-            pltpu.VMEM((2, edge, cells), f32),
-            pltpu.VMEM(flipped, f32),
+            pltpu.VMEM((components, lines, cells), f32),
+            pltpu.VMEM((lines, cells), f32),
+            pltpu.VMEM(y_coef.shape, f32),
+            pltpu.VMEM((2, 8, cells), f32),
+            pltpu.VMEM((2, 8, cells), f32),
+            pltpu.VMEM((LANES, cells), f32),
+            pltpu.VMEM((every, cells, LANES), f32),
             pltpu.VMEM((components, lines, cells), f32),
             pltpu.VMEM((components,) + flipped, f32),
-            pltpu.VMEM((length,) + tiles, f32),
-            pltpu.VMEM((length,) + tiles, f32),
-            pltpu.VMEM((length,) + tiles, f32),
+            pltpu.VMEM((cells, LANES), f32),
+            pltpu.VMEM((length, every, SEGMENTS, LANES), f32),
+            pltpu.VMEM((length, every, SEGMENTS, LANES), f32),
+            pltpu.VMEM((length, every, SEGMENTS, LANES), f32),
             pltpu.VMEM((components, length) + tiles, f32),
+            pltpu.VMEM((length, SEGMENTS, LANES), f32),
             pltpu.VMEM((2 * fields, SEGMENTS * 8, LANES), f32),
             pltpu.VMEM((groups, up8(2 * components), LANES), f32),
             pltpu.VMEM((fields,) + flipped, f32),
             pltpu.VMEM((fields, lines, cells), f32),
             pltpu.VMEM((8, -(-rows // LANES) * LANES), f32),
-            pltpu.VMEM((8, LANES), f32),
             pltpu.VMEM((rows_a, LANES), f32),
             pltpu.VMEM((rows_b, LANES), f32),
+            pltpu.VMEM((8, LANES), f32),
             pltpu.VMEM((peers, rows_a, LANES), f32),
             pltpu.VMEM((peers, rows_b, LANES), f32),
+            pltpu.VMEM((peers, 8, LANES), f32),
+            pltpu.SemaphoreType.DMA((3,)),
             pltpu.SemaphoreType.DMA((2,)),
             pltpu.SemaphoreType.DMA((2,)),
-            pltpu.SemaphoreType.DMA((peers,)),
-            pltpu.SemaphoreType.DMA((peers,)),
-            pltpu.SemaphoreType.DMA((peers,)),
-            pltpu.SemaphoreType.DMA((peers,)),
-        ],
+        ] + [pltpu.SemaphoreType.DMA((peers,))] * 6,
         compiler_params=pltpu.CompilerParams(
             collective_id=0, has_side_effects=True, vmem_limit_bytes=40 * 1024 * 1024
         ),
         name="implicit_lines",
     )(
-        velocity.reshape(components, lines, cells),
-        viscosity.reshape(lines, cells),
-        y_coef,
+        pltpu.with_memory_space_constraint(velocity.reshape(components, lines, cells), pltpu.HBM),
+        pltpu.with_memory_space_constraint(viscosity.reshape(lines, cells), pltpu.HBM),
+        pltpu.with_memory_space_constraint(y_coef, pltpu.HBM),
     )
     return result.reshape(velocity.shape)
 

time: 16.5 us -> 12.4 us (0.75)
  local copies, waits for them, and re-layouts: 3.96 us -> 1.02 us
  Pallas kernels: 12.4 us -> 11.2 us
    unnamed x7 -> x1, local copies, waits for them, and re-layouts: 3.96 us -> 1.02 us
    pallas_call x1, Pallas kernels: 12.4 us -> 11.2 us  [shards(): pl.pallas_call(functools.partial(kernel, devices, wall_devices, planes),...]
where the time goes in v2:
time: 12.4 us; the launch traced here: 12.2 us
  Pallas kernels  11.2 us (90%)
  local copies, waits for them, and re-layouts  1.02 us (8%)
    pallas_call x1, Pallas kernels, shards(): pl.pallas_call(functools.partial(kernel, devices, wall_devices, planes),...  11.2 us
    unnamed x1, local copies, waits for them, and re-layouts  1.02 us

profile of v2, /device:TPU:0, one launch (start us, length us, event | category | flops | bytes accessed | tf_op | source)
XLA Modules:
  0.0 12.2 jit_solution(3584728744467234139)
XLA Ops:
  0.0 11.2 %implicit_lines.1 = f32[3,384,256]{2,1,0:T(8,128)S(1)} custom-call(f32[3,384,256]{2,1,0:T(8,128)} %bitcast.4, f32[384,256]{1,0:T(8,128)} %bitcast.5, f32[2,192]{1,0:T(2,128)} %coef_hbm.1), custom_call_target="tpu_custom_call" | custom-call | tf_op jit(solution)/shard_map/implicit_lines/pallas_call | solution.py:428
  11.2 1.0 %copy.5 = f32[3,2,192,256]{3,2,1,0:T(8,128)} copy(f32[3,2,192,256]{3,2,1,0:T(8,128)S(1)} %bitcast.3) | data formatting | bytes 2359296

commit v3 on v2

--- a/solution.py
+++ b/solution.py
@@ -110,12 +110,41 @@
 
     loads = [
         pltpu.make_async_copy(source, target, load_sem.at[i])
-        for i, (source, target) in enumerate(((visc_hbm, visc), (vel_hbm, vel), (coef_hbm, coef)))
+        for i, (source, target) in enumerate(((vel_hbm, vel), (visc_hbm, visc), (coef_hbm, coef)))
     ]
     for load in loads:
         load.start()
     bounds = [(c * planes + p, c, p * rows, (p + 1) * rows - 1) for c in range(components) for p in range(planes)]
     loads[0].wait()
+    for at, c, low, high in bounds:
+        rows_out[0, at : at + 1, :] = vel[c, high : high + 1, :]
+        rows_out[1, at : at + 1, :] = vel[c, low : low + 1, :]
+    beside = jnp.where(has_below, 1, 0) + jnp.where(has_above, 1, 0)
+    pl.semaphore_wait(barrier, devices - 1 + beside)
+
+    def wall_copy(side, target):
+        return pltpu.make_async_remote_copy(
+            src_ref=rows_out.at[side], dst_ref=rows_in.at[side],
+            send_sem=wall_send.at[side], recv_sem=wall_recv.at[side],
+            device_id={"wall": target}, device_id_type=MESH)
+
+    @pl.when(has_above)
+    def _():
+        wall_copy(0, wall + 1).start()
+
+    @pl.when(has_below)
+    def _():
+        wall_copy(1, wall - 1).start()
+
+    @pl.when(jnp.logical_not(has_below))
+    def _():
+        rows_in[0] = jnp.zeros(rows_in.shape[1:], jnp.float32)
+
+    @pl.when(jnp.logical_not(has_above))
+    def _():
+        rows_in[1] = jnp.zeros(rows_in.shape[1:], jnp.float32)
+
+    loads[1].wait()
     rim[...] = jnp.ones(rim.shape, jnp.float32)
     for at, c, low, high in bounds:
         rim[at : at + 1, :] = visc[low : low + 1, :]
@@ -123,35 +152,6 @@
     for g in range(groups):
         stiff_t[g] = visc[g * LANES : (g + 1) * LANES, :].T
     stiff_t[groups] = rim[...].T
-
-    loads[1].wait()
-    for at, c, low, high in bounds:
-        rows_out[0, at : at + 1, :] = vel[c, high : high + 1, :]
-        rows_out[1, at : at + 1, :] = vel[c, low : low + 1, :]
-    beside = jnp.where(has_below, 1, 0) + jnp.where(has_above, 1, 0)
-    pl.semaphore_wait(barrier, devices - 1 + beside)
-
-    def wall_copy(side, target):
-        return pltpu.make_async_remote_copy(
-            src_ref=rows_out.at[side], dst_ref=rows_in.at[side],
-            send_sem=wall_send.at[side], recv_sem=wall_recv.at[side],
-            device_id={"wall": target}, device_id_type=MESH)
-
-    @pl.when(has_above)
-    def _():
-        wall_copy(0, wall + 1).start()
-
-    @pl.when(has_below)
-    def _():
-        wall_copy(1, wall - 1).start()
-
-    @pl.when(jnp.logical_not(has_below))
-    def _():
-        rows_in[0] = jnp.zeros(rows_in.shape[1:], jnp.float32)
-
-    @pl.when(jnp.logical_not(has_above))
-    def _():
-        rows_in[1] = jnp.zeros(rows_in.shape[1:], jnp.float32)
 
     def ring_copy(d, source, target, send, recv):
         return pltpu.make_async_remote_copy(
@@ -453,10 +453,10 @@
             pltpu.VMEM((8, -(-rows // LANES) * LANES), f32),
             pltpu.VMEM((rows_a, LANES), f32),
             pltpu.VMEM((rows_b, LANES), f32),
-            pltpu.VMEM((8, LANES), f32),
+            pltpu.VMEM((2, LANES), f32),
             pltpu.VMEM((peers, rows_a, LANES), f32),
             pltpu.VMEM((peers, rows_b, LANES), f32),
-            pltpu.VMEM((peers, 8, LANES), f32),
+            pltpu.VMEM((peers, 2, LANES), f32),
             pltpu.SemaphoreType.DMA((3,)),
             pltpu.SemaphoreType.DMA((2,)),
             pltpu.SemaphoreType.DMA((2,)),

time: 12.4 us -> 12.3 us (level)
  no operation moved by 1% of the time
where the time goes in v3:
time: 12.3 us; the launch traced here: 12.2 us
  Pallas kernels  11.2 us (91%)
  local copies, waits for them, and re-layouts  1.02 us (8%)
    pallas_call x1, Pallas kernels, shards(): pl.pallas_call(functools.partial(kernel, devices, wall_devices, planes),...  11.2 us
    unnamed x1, local copies, waits for them, and re-layouts  1.02 us

profile of v3, /device:TPU:0, one launch (start us, length us, event | category | flops | bytes accessed | tf_op | source)
XLA Modules:
  0.0 12.2 jit_solution(8532683680422051635)
XLA Ops:
  0.0 11.2 %implicit_lines.1 = f32[3,384,256]{2,1,0:T(8,128)S(1)} custom-call(f32[3,384,256]{2,1,0:T(8,128)} %bitcast.4, f32[384,256]{1,0:T(8,128)} %bitcast.5, f32[2,192]{1,0:T(2,128)} %coef_hbm.1), custom_call_target="tpu_custom_call" | custom-call | tf_op jit(solution)/shard_map/implicit_lines/pallas_call | solution.py:428
  11.2 1.0 %copy.5 = f32[3,2,192,256]{3,2,1,0:T(8,128)} copy(f32[3,2,192,256]{3,2,1,0:T(8,128)S(1)} %bitcast.3) | data formatting | bytes 2359296

commit v4 on v3

--- a/solution.py
+++ b/solution.py
@@ -97,23 +97,23 @@
     has_above = wall < wall_devices - 1
 
     barrier = pltpu.get_barrier_semaphore()
-    for d in range(1, devices):
-        pl.semaphore_signal(barrier, inc=1, device_id={"stream": lax.rem(me + d, devices)}, device_id_type=MESH)
-
-    @pl.when(has_below)
-    def _():
-        pl.semaphore_signal(barrier, inc=1, device_id={"wall": wall - 1}, device_id_type=MESH)
-
-    @pl.when(has_above)
-    def _():
-        pl.semaphore_signal(barrier, inc=1, device_id={"wall": wall + 1}, device_id_type=MESH)
-
     loads = [
         pltpu.make_async_copy(source, target, load_sem.at[i])
         for i, (source, target) in enumerate(((vel_hbm, vel), (visc_hbm, visc), (coef_hbm, coef)))
     ]
     for load in loads:
         load.start()
+    @pl.when(has_below)
+    def _():
+        pl.semaphore_signal(barrier, inc=1, device_id={"wall": wall - 1}, device_id_type=MESH)
+
+    @pl.when(has_above)
+    def _():
+        pl.semaphore_signal(barrier, inc=1, device_id={"wall": wall + 1}, device_id_type=MESH)
+
+    for d in range(1, devices):
+        pl.semaphore_signal(barrier, inc=1, device_id={"stream": lax.rem(me + d, devices)}, device_id_type=MESH)
+
     bounds = [(c * planes + p, c, p * rows, (p + 1) * rows - 1) for c in range(components) for p in range(planes)]
     loads[0].wait()
     for at, c, low, high in bounds:

time: 12.3 us -> 12.3 us (level)
  no operation moved by 1% of the time
where the time goes in v4:
time: 12.3 us; the launch traced here: 12.2 us
  Pallas kernels  11.2 us (91%)
  local copies, waits for them, and re-layouts  1.02 us (8%)
    pallas_call x1, Pallas kernels, shards(): pl.pallas_call(functools.partial(kernel, devices, wall_devices, planes),...  11.2 us
    unnamed x1, local copies, waits for them, and re-layouts  1.02 us

profile of v4, /device:TPU:0, one launch (start us, length us, event | category | flops | bytes accessed | tf_op | source)
XLA Modules:
  0.0 12.2 jit_solution(187732709901074138)
XLA Ops:
  0.0 11.2 %implicit_lines.1 = f32[3,384,256]{2,1,0:T(8,128)S(1)} custom-call(f32[3,384,256]{2,1,0:T(8,128)} %bitcast.4, f32[384,256]{1,0:T(8,128)} %bitcast.5, f32[2,192]{1,0:T(2,128)} %coef_hbm.1), custom_call_target="tpu_custom_call" | custom-call | tf_op jit(solution)/shard_map/implicit_lines/pallas_call | solution.py:428
  11.2 1.0 %copy.5 = f32[3,2,192,256]{3,2,1,0:T(8,128)} copy(f32[3,2,192,256]{3,2,1,0:T(8,128)S(1)} %bitcast.3) | data formatting | bytes 2359296
